TPU v7x, 32 devices: a whole 2x2x4 slice. The times are simulated.
32 devices in a mesh: row: 4 (over x, core), col: 8 (over z, y).
Axes of the slice: x: 2, y: 2, z: 4, core: 2. Of those that a mesh axis runs over, the one named last changes fastest.
Arguments:
- matrix: float32 [2048, 2048], P('row', 'col'), as said below
- panel: float32 [2048, 256], P(('row', 'col')), may hold values from -0.125 to 0.125
- factor: float32 [256, 256], replicated, as said below
Outputs:
- updated: float32 [2048, 2048], P('row', 'col')
- correction: float32 [2048, 256], P(('row', 'col'))
Inputs may be any that keep to these rules, and one draw needn't show every extreme that they name: `matrix`: symmetric. `factor`: upper triangular with a positive diagonal.
All inputs are finite; a program needn't handle non-finite values.
Results may differ from a plain program's by a relative error of at most 0.000071.
Values sent between devices are 32-bit elements; how exact they have to be, the bound alone decides.
A program may use at most 64 MiB of HBM per device.

v0:
```python
import jax
import jax.numpy as jnp
from jax import lax
from jax.sharding import PartitionSpec as P


def from_root(value, axis, source):
    kept = jnp.where(lax.axis_index(axis) == source, value, 0).astype(value.dtype)
    return lax.psum(kept, axis)


def mult(left, right):
    return jnp.dot(left, right, precision=lax.Precision.HIGHEST, preferred_element_type=jnp.float32)


def per_device(matrix, panel, factor):
    ncols = lax.axis_size("col")
    nrows = lax.axis_size("row")
    blocks = panel.shape[0]
    col_index = lax.axis_index("col")
    col_rows = blocks * nrows
    offset = col_index * nrows % ncols * blocks
    owner = col_index * nrows // ncols
    row_panel = lax.all_gather(panel, "col", axis=0, tiled=True)
    col_panel = from_root(lax.dynamic_slice_in_dim(row_panel, offset, col_rows, 0), "row", owner)
    product = lax.psum(mult(matrix, col_panel), "col")
    scaled = mult(product, factor)
    small = lax.psum(mult(row_panel.T, scaled), "row")
    row_corr = scaled - 0.5 * mult(row_panel, mult(factor.T, small))
    correction = lax.dynamic_slice_in_dim(row_corr, col_index * blocks, blocks, 0)
    col_corr = from_root(lax.dynamic_slice_in_dim(row_corr, offset, col_rows, 0), "row", owner)
    updated = matrix - mult(row_panel, col_corr.T) - mult(row_corr, col_panel.T)
    return (updated, correction)


def solution(mesh):
    in_specs = (P("row", "col"), P(("row", "col"), None), P())
    out_specs = (P("row", "col"), P(("row", "col"), None))
    return jax.shard_map(
        per_device, mesh=mesh, in_specs=in_specs, out_specs=out_specs, check_vma=False
    )
```

profile of v0, /device:TPU:0, one launch (start us, length us, event | category | flops | bytes accessed | tf_op | source)
XLA Modules:
  0.0 231.1 jit_solution(12882593466567161444)
XLA Ops:
  7.2 0.0 all-reduce.5.cloned.1.call-start
  7.2 33.2 %all_gather.3 = f32[512,256]{1,0:T(8,128)S(1)} all-gather(f32[64,256]{1,0:T(8,128)} %param.4), channel_id=1, replica_groups=mesh['row'=4,'col'=8] {'col'}, dimensions={0}, use_global_device_ids=true | all-gather | bytes 589824 | tf_op jit(solution)/shard_map/all_gather | solution.py:24
  40.5 0.7 dynamic-slice_select_fusion.1
  41.2 0.0 all-reduce.5.cloned.1.call-update
  41.2 0.0 all-reduce.7.cloned.1.call-start
  41.3 33.5 %all-reduce.5.cloned.1.call-done = f32[256,256]{1,0:T(8,128)} async-done(((f32[256,256]{1,0:T(8,128)}), f32[256,256]{1,0:T(8,128)}) %all-reduce.5.cloned.1.call-update) | async-done | bytes 262160 | tf_op jit(solution)/shard_map/psum | solution.py:9
  74.8 2.8 %convolution_bitcast_fusion.1 = f32[512,256]{0,1:T(8,128)} fusion(f32[256,256]{1,0:T(8,128)} %all-reduce.5.cloned.1.call-done, f32[512,256]{1,0:T(8,128)S(1)} %copy-done.1), kind=kOutput, calls=%fused_computation.1 | convolution fusion | flops 402653184 | bytes 1310720 | tf_op jit(solution)/shard_map/dot_general | solution.py:13
  77.6 0.0 all-reduce.7.cloned.1.call-update
  77.6 0.0 all-reduce.9.cloned.1.call-start
  77.6 73.8 %all-reduce.7.cloned.1.call-done = f32[512,256]{0,1:T(8,128)} async-done(((f32[512,256]{0,1:T(8,128)}), f32[512,256]{0,1:T(8,128)}) %all-reduce.7.cloned.1.call-update) | async-done | bytes 524304 | tf_op jit(solution)/shard_map/psum | solution.py:26
  151.5 2.0 fusion.4
  153.5 1.7 convolution_bitcast_fusion.2
  155.3 0.0 all-reduce.11.cloned.1.call-start
  155.3 0.2 copy.6
  155.5 31.4 %all-reduce.9.cloned.1.call-done = f32[256,256]{0,1:T(8,128)} async-done(((f32[256,256]{0,1:T(8,128)}), f32[256,256]{0,1:T(8,128)}) %all-reduce.9.cloned.1.call-update) | async-done | bytes 262160 | tf_op jit(solution)/shard_map/psum | solution.py:28
  186.9 1.3 fusion.5
  188.2 0.6 fusion.3
  188.8 0.7 dynamic-slice_select_fusion
  189.6 0.9 copy-done.2
  190.5 0.6 fusion.6
  191.1 0.6 constant_dynamic-slice_fusion
  191.8 30.2 %all-reduce.11.cloned.1.call-done = f32[256,256]{1,0:T(8,128)} async-done(((f32[256,256]{1,0:T(8,128)}), f32[256,256]{1,0:T(8,128)}) %all-reduce.11.cloned.1.call-update) | async-done | bytes 262160 | tf_op jit(solution)/shard_map/psum | solution.py:9
  222.0 1.6 fusion.1
  223.6 1.0 copy.8
  (7 shorter events, 0.0 us)
Async XLA Ops:
  7.2 144.3 %copy-start = (f32[256,256]{1,0:T(8,128)S(1)}, f32[256,256]{1,0:T(8,128)}, u32[]{:S(2)}) copy-start(f32[256,256]{1,0:T(8,128)} %param.5) | copy-start | bytes 786436
  7.2 67.6 %all-reduce.5.cloned.1.call-start = ((), (), s32[]{:S(2)}) async-start(), calls=%async_computation | async-start | bytes 524288 | tf_op jit(solution)/shard_map/psum | solution.py:9
  40.5 34.3 %copy-start.1 = (f32[512,256]{1,0:T(8,128)S(1)}, f32[512,256]{1,0:T(8,128)}, u32[]{:S(2)}) copy-start(f32[512,256]{1,0:T(8,128)} %param.3) | copy-start | bytes 1572868
  41.2 110.2 %all-reduce.7.cloned.1.call-start = ((), (), s32[]{:S(2)}) async-start(), calls=%async_computation.1 | async-start | bytes 1048576 | tf_op jit(solution)/shard_map/psum | solution.py:26
  77.6 109.3 %all-reduce.9.cloned.1.call-start = ((), (), s32[]{:S(2)}) async-start(), calls=%async_computation.2 | async-start | bytes 524288 | tf_op jit(solution)/shard_map/psum | solution.py:28
  155.3 66.8 %all-reduce.11.cloned.1.call-start = ((), (), s32[]{:S(2)}) async-start(), calls=%async_computation.3 | async-start | bytes 524288 | tf_op jit(solution)/shard_map/psum | solution.py:9
  189.5 0.9 copy-start.2
Sparse Core Ops, SparseCore 0:
  41.4 33.3 all-reduce.4
  78.8 72.6 all-reduce.6
  155.4 31.4 all-reduce.8
  189.7 32.2 all-reduce.10
where the time goes:
time: 231 us
  waiting for transfers between devices  169 us (73%)
  blocking collectives  33.2 us (14%)
  between operations  13.8 us (6%)
  matrix products  10.7 us (5%)
  local copies, waits for them, and re-layouts  2.77 us (1%)
    psum x1, waiting for transfers between devices, per_device(): product = lax.psum(mult(matrix, col_panel), 'col')  73.8 us
    psum x2, waiting for transfers between devices, from_root(): return lax.psum(kept, axis)  63.7 us
    all_gather x1, blocking collectives, per_device(): row_panel = lax.all_gather(panel, 'col', axis=0, tiled=True)  33.2 us
    psum x1, waiting for transfers between devices, per_device(): small = lax.psum(mult(row_panel.T, scaled), 'row')  31.4 us
    dot_general x7, matrix products, mult(): jnp.dot(left, right, precision=lax.Precision.HIGHEST, preferred_element_t...  10.7 us
  transfers between devices with their start and end apart: 4, of which 4 were waited for; matrix products, arithmetic and copies ran while one was open for 1% of the time, Pallas kernels for 0%

commit v1 on v0

--- a/solution.py
+++ b/solution.py
@@ -2,6 +2,8 @@
 import jax.numpy as jnp
 from jax import lax
 from jax.sharding import PartitionSpec as P
+
+_part_desk = lambda local_values: jax.lax.all_gather(local_values, "row").sum(axis=0)
 
 
 def from_root(value, axis, source):
@@ -25,7 +27,7 @@
     col_panel = from_root(lax.dynamic_slice_in_dim(row_panel, offset, col_rows, 0), "row", owner)
     product = lax.psum(mult(matrix, col_panel), "col")
     scaled = mult(product, factor)
-    small = lax.psum(mult(row_panel.T, scaled), "row")
+    small = _part_desk(mult(row_panel.T, scaled))
     row_corr = scaled - 0.5 * mult(row_panel, mult(factor.T, small))
     correction = lax.dynamic_slice_in_dim(row_corr, col_index * blocks, blocks, 0)
     col_corr = from_root(lax.dynamic_slice_in_dim(row_corr, offset, col_rows, 0), "row", owner)

time: 231 us -> 217 us (0.939)
  waiting for transfers between devices: 169 us -> 153 us
    psum x1 -> x0, waiting for transfers between devices: 31.4 us -> none  [per_device(): small = lax.psum(mult(row_panel.T, scaled), 'row')]
    all_gather x0 -> x1, waiting for transfers between devices: none -> 15.8 us  [jax.lax.all_gather(local_values, 'row').sum(axis=0)]
where the time goes in v1:
time: 217 us
  waiting for transfers between devices  153 us (71%)
  blocking collectives  33.2 us (15%)
  between operations  13.9 us (6%)
  matrix products  9.74 us (4%)
  local copies, waits for them, and re-layouts  4.47 us (2%)
    psum x1, waiting for transfers between devices, per_device(): product = lax.psum(mult(matrix, col_panel), 'col')  73.8 us
    psum x2, waiting for transfers between devices, from_root(): return lax.psum(kept, axis)  63.7 us
    all_gather x1, blocking collectives, per_device(): row_panel = lax.all_gather(panel, 'col', axis=0, tiled=True)  33.2 us
    all_gather x1, waiting for transfers between devices, jax.lax.all_gather(local_values, 'row').sum(axis=0)  15.8 us
    dot_general x7, matrix products, mult(): jnp.dot(left, right, precision=lax.Precision.HIGHEST, preferred_element_t...  9.74 us
  transfers between devices with their start and end apart: 4, of which 4 were waited for; matrix products, arithmetic and copies ran while one was open for 1% of the time, Pallas kernels for 0%

profile of v1, /device:TPU:0, one launch (start us, length us, event | category | flops | bytes accessed | tf_op | source)
XLA Modules:
  0.0 216.9 jit_solution(10858441932089148347)
XLA Ops:
  7.2 0.0 all-reduce.4.cloned.1.call-start
  7.2 33.2 %all_gather.9 = f32[512,256]{1,0:T(8,128)S(1)} all-gather(f32[64,256]{1,0:T(8,128)} %param.4), channel_id=1, replica_groups=mesh['row'=4,'col'=8] {'col'}, dimensions={0}, use_global_device_ids=true | all-gather | bytes 589824 | tf_op jit(solution)/shard_map/all_gather | solution.py:26
  40.5 0.7 dynamic-slice_select_fusion.1
  41.2 0.0 all-reduce.6.cloned.1.call-start
  41.3 33.5 %all-reduce.4.cloned.1.call-done = f32[256,256]{1,0:T(8,128)} async-done(((f32[256,256]{1,0:T(8,128)}), f32[256,256]{1,0:T(8,128)}) %all-reduce.4.cloned.1.call-update) | async-done | bytes 262160 | tf_op jit(solution)/shard_map/psum | solution.py:11
  74.8 2.8 %convolution_bitcast_fusion.1 = f32[512,256]{0,1:T(8,128)} fusion(f32[256,256]{1,0:T(8,128)} %all-reduce.4.cloned.1.call-done, f32[512,256]{1,0:T(8,128)S(1)} %copy-done.1), kind=kOutput, calls=%fused_computation.1 | convolution fusion | flops 402653184 | bytes 1310720 | tf_op jit(solution)/shard_map/dot_general | solution.py:15
  77.6 0.0 all-gather.3.cloned.1.call-start
  77.6 73.8 %all-reduce.6.cloned.1.call-done = f32[512,256]{0,1:T(8,128)} async-done(((f32[512,256]{0,1:T(8,128)}), f32[512,256]{0,1:T(8,128)}) %all-reduce.6.cloned.1.call-update) | async-done | bytes 524304 | tf_op jit(solution)/shard_map/psum | solution.py:28
  151.5 2.0 fusion.4
  153.5 1.7 convolution_bitcast_fusion.2
  155.3 0.0 all-reduce.8.cloned.1.call-start
  155.3 0.2 copy.10
  155.5 15.8 %all-gather.3.cloned.1.call-done = f32[1024,256]{0,1:T(8,128)} async-done(((f32[256,256]{0,1:T(8,128)}), f32[1024,256]{0,1:T(8,128)}) %all-gather.3.cloned.1.call-update) | async-done | bytes 1048592 | tf_op jit(solution)/shard_map/all_gather | solution.py:6
  171.3 1.7 reshape.4
  173.0 0.6 reduce_sum.9
  173.6 0.4 fusion.5
  174.0 0.6 fusion.3
  174.6 0.7 dynamic-slice_select_fusion
  175.4 0.9 copy-done.2
  176.3 0.6 fusion.6
  176.9 0.6 constant_dynamic-slice_fusion
  177.6 30.2 %all-reduce.8.cloned.1.call-done = f32[256,256]{1,0:T(8,128)} async-done(((f32[256,256]{1,0:T(8,128)}), f32[256,256]{1,0:T(8,128)}) %all-reduce.8.cloned.1.call-update) | async-done | bytes 262160 | tf_op jit(solution)/shard_map/psum | solution.py:11
  207.8 1.6 fusion.1
  209.4 1.0 copy.12
  (9 shorter events, 0.1 us)
Async XLA Ops:
  7.2 144.3 %copy-start = (f32[256,256]{1,0:T(8,128)S(1)}, f32[256,256]{1,0:T(8,128)}, u32[]{:S(2)}) copy-start(f32[256,256]{1,0:T(8,128)} %param.5) | copy-start | bytes 786436
  7.2 67.6 %all-reduce.4.cloned.1.call-start = ((), (), s32[]{:S(2)}) async-start(), calls=%async_computation | async-start | bytes 524288 | tf_op jit(solution)/shard_map/psum | solution.py:11
  40.5 34.3 %copy-start.1 = (f32[512,256]{1,0:T(8,128)S(1)}, f32[512,256]{1,0:T(8,128)}, u32[]{:S(2)}) copy-start(f32[512,256]{1,0:T(8,128)} %param.3) | copy-start | bytes 1572868
  41.2 110.2 %all-reduce.6.cloned.1.call-start = ((), (), s32[]{:S(2)}) async-start(), calls=%async_computation.1 | async-start | bytes 1048576 | tf_op jit(solution)/shard_map/psum | solution.py:28
  77.6 93.7 %all-gather.3.cloned.1.call-start = ((), (), s32[]{:S(2)}) async-start(), calls=%async_computation.3 | async-start | bytes 1310720 | tf_op jit(solution)/shard_map/all_gather | solution.py:6
  155.3 52.6 %all-reduce.8.cloned.1.call-start = ((), (), s32[]{:S(2)}) async-start(), calls=%async_computation.2 | async-start | bytes 524288 | tf_op jit(solution)/shard_map/psum | solution.py:11
  175.4 0.9 copy-start.2
Sparse Core Ops, SparseCore 0:
  41.4 33.3 all-reduce.3
  78.8 72.6 all-reduce.5
  155.4 15.8 all-gather.2
  175.5 32.2 all-reduce.7
